TPU v7x, 32 devices: a whole 2x2x4 slice. The times are simulated.
32 devices in a mesh: batch: 4 (over z), seq: 8 (over y, x, core).
Axes of the slice: x: 2, y: 2, z: 4, core: 2. Of those that a mesh axis runs over, the one named last changes fastest.
Arguments:
- inputs: float32 [8, 1024, 768], P('batch', 'seq'), may hold values from -6 to 6
- cotangent: float32 [8, 1024, 768], P('batch', 'seq'), may hold values from -6 to 6
- lengths: int32 [8], P('batch'), may hold values from 256 to 1024, as said below
- joint_weight: bfloat16 [768, 2304], P(('batch', 'seq')), may hold values from -0.3125 to 0.3125
- output_weight: bfloat16 [768, 768], P(('batch', 'seq')), may hold values from -1.25 to 1.25
- vectors: bfloat16 [8, 768], P(None, ('batch', 'seq')), may hold values from -2 to 2
- expand_weight: bfloat16 [768, 3072], P(('batch', 'seq')), may hold values from -0.21875 to 0.21875
- expand_bias: bfloat16 [3072], P(('batch', 'seq')), may hold values from -1.1953125 to 1.1953125
- reduce_weight: bfloat16 [3072, 768], P(('batch', 'seq')), may hold values from -0.15625 to 0.15625
Outputs:
- result: float32 [8, 1024, 768], P('batch', 'seq')
- grad_inputs: float32 [8, 1024, 768], P('batch', 'seq')
- grad_joint: float32 [768, 2304], P(('batch', 'seq'))
- grad_output: float32 [768, 768], P(('batch', 'seq'))
- grad_vectors: float32 [8, 768], P(None, ('batch', 'seq'))
- grad_expand: float32 [768, 3072], P(('batch', 'seq'))
- grad_expand_bias: float32 [3072], P(('batch', 'seq'))
- grad_reduce: float32 [3072, 768], P(('batch', 'seq'))
Inputs may be any that keep to these rules, and one draw needn't show every extreme that they name: `lengths`: some sequence is full (1024 valid tokens) in every draw.
All inputs are finite; a program needn't handle non-finite values.
Results may differ from a plain program's by a relative error of at most 0.018.
The roundings to bfloat16 on the way count: a program that leaves them out, or rounds other values in their place, can miss the bound.
Values may be sent and summed in bfloat16 or wider, within the bound.
A program may use at most 192 MiB of HBM per device.

v0:
```python
import math
import jax
import jax.numpy as jnp
from jax import lax
from jax.sharding import PartitionSpec as P

HEADS = 12
HEAD_DIM = 64
EPSILON = 1e-12
SCORE_SCALE = 0.125
NEG_FILL = -1e30
HALF_ROOT = 0.7071067811865476
INV_ROOT_TAU = 0.3989422804014327
block_limit = 256


def layer_norm(residual, norm_gain, norm_shift):
    centered = residual - jnp.mean(residual, axis=-1, keepdims=True)
    inverse = lax.rsqrt(jnp.mean(centered * centered, axis=-1, keepdims=True) + EPSILON)
    normed = centered * inverse
    return (normed * norm_gain + norm_shift, normed, inverse)


def norm_back(grad_out, normed, inverse, norm_gain):
    grad_normed = grad_out * norm_gain
    mean_grad = jnp.mean(grad_normed, axis=-1, keepdims=True)
    mean_proj = jnp.mean(grad_normed * normed, axis=-1, keepdims=True)
    grad_in = inverse * (grad_normed - mean_grad - normed * mean_proj)
    return (grad_in, jnp.sum(grad_out * normed, axis=0), jnp.sum(grad_out, axis=0))


def gelu_value(before_gelu):
    return 0.5 * before_gelu * (1.0 + lax.erf(before_gelu * HALF_ROOT))


def gelu_slope(before_gelu):
    return (
        0.5 * (1.0 + lax.erf(before_gelu * HALF_ROOT))
        + before_gelu * jnp.exp(-0.5 * before_gelu * before_gelu) * INV_ROOT_TAU
    )


def over_blocks(piece_rows, block_fn, carried):
    block_size = math.gcd(piece_rows, block_limit)

    def run_block(block_index, current):
        return block_fn(current, block_index * block_size, block_size)

    return lax.fori_loop(0, piece_rows // block_size, run_block, carried)


def head_scores(left_heads, right_heads, right_places, lengths):
    scores = (
        jnp.einsum("sqhd,skhd->shqk", left_heads, right_heads, preferred_element_type=jnp.float32)
        * SCORE_SCALE
    )
    allowed = right_places[None, :] < lengths[:, None]
    return jnp.where(allowed[:, None, None, :], scores, NEG_FILL)


def cut_heads(gathered_piece, offset, block_size, head_count):
    sliced = lax.dynamic_slice_in_dim(gathered_piece, offset, block_size, 1)
    return sliced.reshape(sliced.shape[0], block_size, head_count, -1)


def gather_attention(joint_weight, output_weight, vectors):
    return (
        lax.all_gather(joint_weight, ("batch", "seq"), axis=0, tiled=True),
        lax.all_gather(output_weight, ("batch", "seq"), axis=0, tiled=True),
        lax.all_gather(vectors, ("batch", "seq"), axis=1, tiled=True),
    )


def gather_feed(expand_weight, reduce_weight, expand_bias):
    return (
        lax.all_gather(expand_weight, ("batch", "seq"), axis=0, tiled=True),
        lax.all_gather(reduce_weight, ("batch", "seq"), axis=0, tiled=True),
        lax.all_gather(expand_bias, ("batch", "seq"), axis=0, tiled=True),
    )


def on_device(
    inputs,
    cotangent,
    lengths,
    joint_weight,
    output_weight,
    vectors,
    expand_weight,
    expand_bias,
    reduce_weight,
):
    seq_count, row_count, model_width = inputs.shape
    head_count = HEADS
    head_size = HEAD_DIM
    tokens = seq_count * row_count
    head_shape = (seq_count, row_count, head_count, head_size)
    own_places = lax.axis_index("seq") * row_count + jnp.arange(row_count, dtype=jnp.int32)
    row_valid = own_places[None, :] < lengths[:, None]
    row_mask = row_valid.reshape(tokens, 1).astype(jnp.float32)
    full_joint, full_output, full_vectors = gather_attention(joint_weight, output_weight, vectors)
    vector_rows = full_vectors.astype(jnp.float32)
    flat_inputs = inputs.reshape(tokens, model_width)
    input_low = flat_inputs.astype(jnp.bfloat16)
    projected = jnp.dot(input_low, full_joint, preferred_element_type=jnp.float32)
    query_low = (projected[:, :model_width] + vector_rows[2]).astype(jnp.bfloat16)
    key_low = projected[:, model_width : 2 * model_width].astype(jnp.bfloat16)
    value_low = (projected[:, 2 * model_width :] + vector_rows[3]).astype(jnp.bfloat16)
    query_heads = query_low.reshape(head_shape)
    key_rows = key_low.reshape(seq_count, row_count, model_width)
    value_rows = value_low.reshape(seq_count, row_count, model_width)
    start_state = (
        jnp.full((seq_count, head_count, row_count), NEG_FILL, jnp.float32),
        jnp.zeros((seq_count, head_count, row_count), jnp.float32),
        jnp.zeros(head_shape, jnp.float32),
    )
    key_piece = lax.all_gather(key_rows, "seq", axis=1, tiled=True)
    value_piece = lax.all_gather(value_rows, "seq", axis=1, tiled=True)

    def forward_score_block(current, offset, block_size):
        running_max, running_sum, summed = current
        key_heads = cut_heads(key_piece, offset, block_size, head_count)
        value_heads = cut_heads(value_piece, offset, block_size, head_count)
        key_places = offset + jnp.arange(block_size, dtype=jnp.int32)
        scores = head_scores(query_heads, key_heads, key_places, lengths)
        new_max = jnp.maximum(running_max, jnp.max(scores, axis=-1))
        factor = jnp.exp(running_max - new_max)
        exp_scores = jnp.exp(scores - new_max[..., None])
        running_sum = running_sum * factor + jnp.sum(exp_scores, axis=-1)
        update = jnp.einsum(
            "shqk,skhd->sqhd",
            exp_scores.astype(jnp.bfloat16),
            value_heads,
            preferred_element_type=jnp.float32,
        )
        summed = summed * jnp.transpose(factor, (0, 2, 1))[..., None] + update
        return (new_max, running_sum, summed)

    running_max, running_sum, summed = over_blocks(
        key_piece.shape[1], forward_score_block, start_state
    )
    attended = summed / jnp.transpose(running_sum, (0, 2, 1))[..., None]
    log_total = jnp.transpose(running_max + jnp.log(running_sum), (0, 2, 1))
    context_low = attended.reshape(tokens, model_width).astype(jnp.bfloat16)
    branch = jnp.dot(context_low, full_output, preferred_element_type=jnp.float32) + vector_rows[4]
    first, first_normed, first_inverse = layer_norm(
        flat_inputs + branch, vector_rows[0], vector_rows[1]
    )
    first_low = first.astype(jnp.bfloat16)
    full_expand, full_reduce, full_bias = gather_feed(expand_weight, reduce_weight, expand_bias)
    before_gelu = jnp.dot(
        first_low, full_expand, preferred_element_type=jnp.float32
    ) + full_bias.astype(jnp.float32)
    hidden_low = gelu_value(before_gelu).astype(jnp.bfloat16)
    feed = jnp.dot(hidden_low, full_reduce, preferred_element_type=jnp.float32) + vector_rows[7]
    result, second_normed, second_inverse = layer_norm(first + feed, vector_rows[5], vector_rows[6])
    full_expand, full_reduce, full_bias = gather_feed(expand_weight, reduce_weight, expand_bias)
    full_joint, full_output, full_vectors = gather_attention(joint_weight, output_weight, vectors)
    grad_res = cotangent.reshape(tokens, model_width) * row_mask
    grad_second, grad_gain_two, grad_shift_two = norm_back(
        grad_res, second_normed, second_inverse, vector_rows[5]
    )
    grad_feed_low = grad_second.astype(jnp.bfloat16)
    grad_reduce_local = jnp.dot(hidden_low.T, grad_feed_low, preferred_element_type=jnp.float32)
    grad_hidden = jnp.dot(
        grad_feed_low, full_reduce.T, preferred_element_type=jnp.float32
    ) * gelu_slope(before_gelu)
    grad_hidden_low = grad_hidden.astype(jnp.bfloat16)
    grad_expand_local = jnp.dot(first_low.T, grad_hidden_low, preferred_element_type=jnp.float32)
    grad_bias_local = jnp.sum(grad_hidden_low.astype(jnp.float32), axis=0)
    grad_first = grad_second + jnp.dot(
        grad_hidden_low, full_expand.T, preferred_element_type=jnp.float32
    )
    grad_resid, grad_gain_one, grad_shift_one = norm_back(
        grad_first, first_normed, first_inverse, vector_rows[0]
    )
    grad_branch_low = grad_resid.astype(jnp.bfloat16)
    grad_output_local = jnp.dot(context_low.T, grad_branch_low, preferred_element_type=jnp.float32)
    grad_context_low = jnp.dot(
        grad_branch_low, full_output.T, preferred_element_type=jnp.float32
    ).astype(jnp.bfloat16)
    grad_context_heads = grad_context_low.reshape(head_shape)
    row_delta = jnp.sum(grad_context_heads.astype(jnp.float32) * attended, axis=-1)
    log_heads = jnp.transpose(log_total, (0, 2, 1))
    delta_heads = jnp.transpose(row_delta, (0, 2, 1))
    query_key_piece = lax.all_gather(key_rows, "seq", axis=1, tiled=True)
    query_value_piece = lax.all_gather(value_rows, "seq", axis=1, tiled=True)

    def query_score_block(current, offset, block_size):
        key_heads = cut_heads(query_key_piece, offset, block_size, head_count)
        value_heads = cut_heads(query_value_piece, offset, block_size, head_count)
        key_places = offset + jnp.arange(block_size, dtype=jnp.int32)
        scores = head_scores(query_heads, key_heads, key_places, lengths)
        softmax_rows = jnp.exp(scores - log_heads[..., None])
        grad_probs = jnp.einsum(
            "sqhd,skhd->shqk", grad_context_heads, value_heads, preferred_element_type=jnp.float32
        )
        grad_scores = (softmax_rows * (grad_probs - delta_heads[..., None])).astype(jnp.bfloat16)
        return (
            current
            + jnp.einsum(
                "shqk,skhd->sqhd", grad_scores, key_heads, preferred_element_type=jnp.float32
            )
            * SCORE_SCALE
        )

    grad_query = over_blocks(
        query_key_piece.shape[1], query_score_block, jnp.zeros(head_shape, jnp.float32)
    )
    own_keys = key_low.reshape(head_shape)
    own_values = value_low.reshape(head_shape)
    query_rows = query_low.reshape(seq_count, row_count, model_width)
    grad_context_rows = grad_context_low.reshape(seq_count, row_count, model_width)
    zero_heads = jnp.zeros(head_shape, jnp.float32)
    query_piece = lax.all_gather(query_rows.astype(jnp.float32), "seq", axis=1, tiled=True).astype(
        jnp.bfloat16
    )
    grad_piece = lax.all_gather(
        grad_context_rows.astype(jnp.float32), "seq", axis=1, tiled=True
    ).astype(jnp.bfloat16)
    log_piece = lax.all_gather(log_total, "seq", axis=1, tiled=True)
    delta_piece = lax.all_gather(row_delta, "seq", axis=1, tiled=True)

    def key_score_block(current, offset, block_size):
        grad_key, grad_value = current
        query_block = cut_heads(query_piece, offset, block_size, head_count)
        grad_block = cut_heads(grad_piece, offset, block_size, head_count)
        log_block = jnp.transpose(
            lax.dynamic_slice_in_dim(log_piece, offset, block_size, 1), (0, 2, 1)
        )
        delta_block = jnp.transpose(
            lax.dynamic_slice_in_dim(delta_piece, offset, block_size, 1), (0, 2, 1)
        )
        scores = head_scores(query_block, own_keys, own_places, lengths)
        softmax_rows = jnp.exp(scores - log_block[..., None])
        grad_value = grad_value + jnp.einsum(
            "shqk,sqhd->skhd",
            softmax_rows.astype(jnp.bfloat16),
            grad_block,
            preferred_element_type=jnp.float32,
        )
        grad_probs = jnp.einsum(
            "sqhd,skhd->shqk", grad_block, own_values, preferred_element_type=jnp.float32
        )
        grad_scores = (softmax_rows * (grad_probs - delta_block[..., None])).astype(jnp.bfloat16)
        grad_key = (
            grad_key
            + jnp.einsum(
                "shqk,sqhd->skhd", grad_scores, query_block, preferred_element_type=jnp.float32
            )
            * SCORE_SCALE
        )
        return (grad_key, grad_value)

    grad_key, grad_value = over_blocks(
        query_piece.shape[1], key_score_block, (zero_heads, zero_heads)
    )
    grad_query_low = grad_query.reshape(tokens, model_width).astype(jnp.bfloat16)
    grad_key_low = grad_key.reshape(tokens, model_width).astype(jnp.bfloat16)
    grad_value_low = grad_value.reshape(tokens, model_width).astype(jnp.bfloat16)
    grad_projected = jnp.concatenate([grad_query_low, grad_key_low, grad_value_low], axis=1)
    grad_joint_local = jnp.dot(input_low.T, grad_projected, preferred_element_type=jnp.float32)
    grad_inputs = grad_resid + jnp.dot(
        grad_projected, full_joint.T, preferred_element_type=jnp.float32
    )
    grad_vector_local = jnp.stack(
        [
            grad_gain_one,
            grad_shift_one,
            jnp.sum(grad_query_low.astype(jnp.float32), axis=0),
            jnp.sum(grad_value_low.astype(jnp.float32), axis=0),
            jnp.sum(grad_branch_low.astype(jnp.float32), axis=0),
            grad_gain_two,
            grad_shift_two,
            jnp.sum(grad_feed_low.astype(jnp.float32), axis=0),
        ],
        axis=0,
    )
    every_grad = (
        lax.psum_scatter(grad_joint_local, ("batch", "seq"), scatter_dimension=0, tiled=True),
        lax.psum_scatter(grad_output_local, ("batch", "seq"), scatter_dimension=0, tiled=True),
        lax.psum_scatter(grad_vector_local, ("batch", "seq"), scatter_dimension=1, tiled=True),
        lax.psum_scatter(grad_expand_local, ("batch", "seq"), scatter_dimension=0, tiled=True),
        lax.psum_scatter(grad_reduce_local, ("batch", "seq"), scatter_dimension=0, tiled=True),
        lax.psum_scatter(grad_bias_local, ("batch", "seq"), scatter_dimension=0, tiled=True),
    )
    summed_grads = (
        every_grad[0],
        every_grad[1],
        every_grad[2],
        every_grad[3],
        every_grad[5],
        every_grad[4],
    )
    return (
        result.reshape(seq_count, row_count, model_width),
        grad_inputs.reshape(seq_count, row_count, model_width),
        summed_grads[0],
        summed_grads[1],
        summed_grads[2],
        summed_grads[3],
        summed_grads[4],
        summed_grads[5],
    )


def solution(mesh):
    return jax.shard_map(
        on_device,
        mesh=mesh,
        in_specs=(
            P("batch", "seq", None),
            P("batch", "seq", None),
            P("batch"),
            P(("batch", "seq"), None),
            P(("batch", "seq"), None),
            P(None, ("batch", "seq")),
            P(("batch", "seq"), None),
            P(("batch", "seq")),
            P(("batch", "seq"), None),
        ),
        out_specs=(
            P("batch", "seq", None),
            P("batch", "seq", None),
            P(("batch", "seq"), None),
            P(("batch", "seq"), None),
            P(None, ("batch", "seq")),
            P(("batch", "seq"), None),
            P(("batch", "seq")),
            P(("batch", "seq"), None),
        ),
        check_vma=False,
    )
```

profile of v0, /device:TPU:0, one launch (start us, length us, event | category | flops | bytes accessed | tf_op | source)
XLA Modules:
  0.0 933.9 jit_solution(14947603904513098469)
XLA Ops:
  9.1 64.5 %all-gather.10.cloned.1.call-done = bf16[768,2304]{1,0:T(8,128)(2,1)} async-done(((bf16[24,2304]{1,0:T(8,128)(2,1)}), bf16[768,2304]{1,0:T(8,128)(2,1)}) %all-gather.10.cloned.1.call-update) | async-done | bytes 3538960 | tf_op jit(solution)/shard_map/all_gather | solution.py:68
  77.9 42.5 %all-gather = bf16[32,24,8]{1,2,0:T(8,128)(2,1)} all-gather(bf16[1,24,8]{1,2,0:T(8,128)(2,1)S(1)} %bitcast.230), channel_id=1, replica_groups=mesh['batch'=4,'seq'=8] {'batch','seq'}, dimensions={0}, use_global_device_ids=true | all-gather | bytes 12672 | tf_op jit(solution)/shard_map/all_gather | solution.py:70
  131.3 37.1 %all-reduce = bf16[3072]{0:T(1024)(128)(2,1)S(1)} all-reduce(bf16[3072]{0:T(1024)(128)(2,1)S(1)} %dynamic-update-slice), channel_id=1, replica_groups=mesh['batch'=4,'seq'=8] {'batch','seq'}, use_global_device_ids=true, to_apply=%add | all-reduce | flops 3072 | bytes 12288
  175.0 38.4 %while.48 = (s32[]{:T(128)}, f32[2,12,128]{2,1,0:T(8,128)S(1)}, f32[2,12,128]{2,1,0:T(8,128)}, f32[2,128,12,64]{1,3,2,0:T(8,128)}, s32[2]{0:T(128)}, /*index=5*/...) while((s32[]{:T(128)}, f32[2,12,128]{2,1,0:T(8,128)S(1)}, ...), condition=%wide.region_3.4_spmd.clone, body=%wide.region_0.3_spmd.clone.sunk | while | flops 210586368 | bytes 25862536 | solution.py:49
  219.4 60.8 %all-gather.18.cloned.1.call-done = bf16[768,3072]{1,0:T(8,128)(2,1)} async-done(((bf16[24,3072]{1,0:T(8,128)(2,1)}), bf16[768,3072]{1,0:T(8,128)(2,1)}) %all-gather.18.cloned.1.call-update) | async-done | bytes 4718608 | tf_op jit(solution)/shard_map/all_gather | solution.py:76
  280.2 6.1 multiply_convert_fusion.2
  286.3 59.1 %all-gather.20.cloned.1.call-done = bf16[3072,768]{1,0:T(8,128)(2,1)} async-done(((bf16[96,768]{1,0:T(8,128)(2,1)}), bf16[3072,768]{1,0:T(8,128)(2,1)}) %all-gather.20.cloned.1.call-update) | async-done | bytes 4718608 | tf_op jit(solution)/shard_map/all_gather | solution.py:77
  345.5 4.4 fusion.75
  362.9 6.7 fusion.70
  375.6 5.1 fusion.66
  380.8 34.9 %while.49 = (s32[]{:T(128)}, f32[2,128,12,64]{1,3,2,0:T(8,128)}, bf16[2,1024,768]{1,2,0:T(8,128)(2,1)}, s32[2]{0:T(128)}, bf16[2,128,12,64]{1,3,2,0:T(8,128)(2,1...) while((s32[]{:T(128)}, f32[2,128,12,64]{1,3,2,0:T(8,128)}, ...), condition=%wide.region_14.15_spmd.clone, body=%wide.region_13.14_spmd.clone.sunk | while | flops 307299072 | bytes 17329384 | solution.py:49
  385.5 3.8 fusion.148
  393.9 4.1 fusion.148
  402.7 4.1 fusion.148
  411.4 4.2 fusion.148
  418.0 10.1 %all_gather.53 = f32[2,1024,12]{1,0,2:T(2,128)} all-gather(f32[2,128,12]{1,0,2:T(2,128)S(1)} %copy-done.29), channel_id=1, replica_groups=mesh['batch'=4,'seq'=8] {'seq'}, dimensions={1}, use_global_device_ids=true | all-gather | bytes 110592 | tf_op jit(solution)/shard_map/all_gather | solution.py:222
  428.1 10.4 %all_gather.51 = f32[2,1024,12]{1,2,0:T(8,128)} all-gather(f32[2,128,12]{1,2,0:T(8,128)} %bitcast.229), channel_id=1, replica_groups=mesh['batch'=4,'seq'=8] {'seq'}, dimensions={1}, use_global_device_ids=true | all-gather | bytes 110592 | tf_op jit(solution)/shard_map/all_gather | solution.py:221
  439.3 57.5 %while.50 = (s32[]{:T(128)}, f32[2,128,12,64]{1,3,2,0:T(8,128)}, f32[2,128,12,64]{1,3,2,0:T(8,128)}, bf16[2,1024,768]{1,2,0:T(8,128)(2,1)}, s32[2]{0:T(128)}, /*...) while((s32[]{:T(128)}, f32[2,128,12,64]{1,3,2,0:T(8,128)}, ...), condition=%wide.region_16.17_spmd.clone, body=%wide.region_15.16_spmd.clone.sunk | while | flops 411500928 | bytes 24602652 | solution.py:49
  445.5 4.7 fusion.157
  459.5 4.9 fusion.157
  464.4 3.4 fusion.158
  474.0 4.9 fusion.157
  478.9 3.4 fusion.158
  488.5 4.9 fusion.157
  493.4 3.4 fusion.158
  500.5 3.9 convolution_bitcast_fusion
  504.4 8.1 copy.96
  513.4 40.3 %all-reduce.3 = (f32[8,768]{1,0:T(8,128)S(1)}, f32[3072]{0:T(1024)S(1)}) all-reduce(f32[8,768]{1,0:T(8,128)S(1)} %stack.35, f32[3072]{0:T(1024)S(1)} %copy-done.41), channel_id=4, replica_groups=mesh['batch'=4,'seq'=8] {'batch','seq'}, use_global_device_ids=true, to_apply=%region_27.28.clone | all-reduce | flops 9216 | bytes 73728
  555.0 4.2 convolution_add_fusion.2
  559.2 101.4 %reduce-scatter.10.cloned.1.call-done = f32[24,3072]{1,0:T(8,128)} async-done(((f32[768,3072]{1,0:T(8,128)}), f32[24,3072]{1,0:T(8,128)}) %reduce-scatter.10.cloned.1.call-update) | async-done | bytes 294928 | tf_op jit(solution)/shard_map/reduce_scatter | solution.py:283
  660.6 140.9 %reduce-scatter.12.cloned.1.call-done = f32[96,768]{1,0:T(8,128)} async-done(((f32[3072,768]{1,0:T(8,128)}), f32[96,768]{1,0:T(8,128)}) %reduce-scatter.12.cloned.1.call-update) | async-done | bytes 294928 | tf_op jit(solution)/shard_map/reduce_scatter | solution.py:284
  801.5 125.5 %reduce-scatter.14.cloned.1.call-done = f32[24,2304]{1,0:T(8,128)} async-done(((f32[768,2304]{1,0:T(8,128)}), f32[24,2304]{1,0:T(8,128)}) %reduce-scatter.14.cloned.1.call-update) | async-done | bytes 221200
  (353 shorter events, 141.7 us)
Async XLA Ops:
  7.2 66.5 %all-gather.10.cloned.1.call-start = ((), (), s32[]{:S(2)}) async-start(), calls=%async_computation.4 | async-start | bytes 3649536 | tf_op jit(solution)/shard_map/all_gather | solution.py:68
  7.9 167.1 %all-gather.12.cloned.1.call-start = ((), (), s32[]{:S(2)}) async-start(), calls=%async_computation.5 | async-start | bytes 3538944 | tf_op jit(solution)/shard_map/all_gather | solution.py:117
  9.1 64.6 %copy-start.9 = (bf16[256,768]{1,0:T(8,128)(2,1)}, bf16[256,768]{1,0:T(8,128)(2,1)S(1)}, u32[]{:S(2)}) copy-start(bf16[256,768]{1,0:T(8,128)(2,1)S(1)} %bitcast_convert_fusion) | copy-start | bytes 1179652
  9.1 68.7 %copy-start.47 = (bf16[8,24]{1,0:T(8,128)(2,1)S(1)}, bf16[8,24]{1,0:T(8,128)(2,1)}, u32[]{:S(2)}) copy-start(bf16[8,24]{1,0:T(8,128)(2,1)} %param.20) | copy-start | bytes 1156
  76.8 93.5 %copy-start.4 = (f32[2,128,768]{2,1,0:T(8,128)S(1)}, f32[2,128,768]{2,1,0:T(8,128)}, u32[]{:S(2)}) copy-start(f32[2,128,768]{2,1,0:T(8,128)} %param.16) | copy-start | bytes 2359300
  76.8 49.9 %copy-start.14 = (bf16[256,768]{1,0:T(8,128)(2,1)}, bf16[256,768]{1,0:T(8,128)(2,1)S(1)}, u32[]{:S(2)}) copy-start(bf16[256,768]{1,0:T(8,128)(2,1)S(1)} %slice.73) | copy-start | bytes 1179652
  77.8 97.2 %all-gather.14.cloned.1.call-start = ((), (), s32[]{:S(2)}) async-start(), calls=%async_computation.6 | async-start | bytes 3538944 | tf_op jit(solution)/shard_map/all_gather | solution.py:118
  127.7 47.3 %copy-start.11 = (bf16[256,768]{1,0:T(8,128)(2,1)}, bf16[256,768]{1,0:T(8,128)(2,1)S(1)}, u32[]{:S(2)}) copy-start(bf16[256,768]{1,0:T(8,128)(2,1)S(1)} %get-tuple-element.821) | copy-start | bytes 1179652
  127.7 46.1 %copy-start.13 = (bf16[256,768]{1,0:T(8,128)(2,1)S(1)}, bf16[256,768]{1,0:T(8,128)(2,1)}, u32[]{:S(2)}) copy-start(bf16[256,768]{1,0:T(8,128)(2,1)} %get-tuple-element.822) | copy-start | bytes 1179652
  128.6 88.4 %all-gather.16.cloned.1.call-start = ((), (), s32[]{:S(2)}) async-start(), calls=%async_computation.7 | async-start | bytes 1216512 | tf_op jit(solution)/shard_map/all_gather | solution.py:69
  129.2 151.0 %all-gather.18.cloned.1.call-start = ((), (), s32[]{:S(2)}) async-start(), calls=%async_computation.8 | async-start | bytes 4866048 | tf_op jit(solution)/shard_map/all_gather | solution.py:76
  129.8 215.7 %all-gather.20.cloned.1.call-start = ((), (), s32[]{:S(2)}) async-start(), calls=%async_computation.9 | async-start | bytes 4866048 | tf_op jit(solution)/shard_map/all_gather | solution.py:77
  130.4 308.9 %all-gather.22.cloned.1.call-start = ((), (), s32[]{:S(2)}) async-start(), calls=%async_computation.10 | async-start | bytes 3538944 | tf_op jit(solution)/shard_map/all_gather | solution.py:215
  174.7 264.6 %all-gather.24.cloned.1.call-start = ((), (), s32[]{:S(2)}) async-start(), calls=%async_computation.11 | async-start | bytes 3538944 | tf_op jit(solution)/shard_map/all_gather | solution.py:218
  213.4 66.8 %copy-start.27 = (f32[768]{0:T(1024)S(1)}, f32[768]{0:T(1024)}, u32[]{:S(2)}) copy-start(f32[768]{0:T(1024)} %get-tuple-element.737) | copy-start | bytes 9220
  213.4 66.8 %copy-start.30 = (f32[768]{0:T(1024)S(1)}, f32[768]{0:T(1024)}, u32[]{:S(2)}) copy-start(f32[768]{0:T(1024)} %get-tuple-element.736) | copy-start | bytes 9220
  213.4 66.8 %copy-start.40 = (f32[3072]{0:T(1024)S(1)}, f32[3072]{0:T(1024)}, u32[]{:S(2)}) copy-start(f32[3072]{0:T(1024)} %convert_element_type.147) | copy-start | bytes 36868
  219.2 139.1 %copy-start.33 = (f32[256]{0:T(256)}, f32[256]{0:T(256)S(1)}, u32[]{:S(2)}) copy-start(f32[256]{0:T(256)S(1)} %broadcast_multiply_fusion.4) | copy-start | bytes 3076
  219.4 138.9 %copy-start.39 = (f32[256]{0:T(256)}, f32[256]{0:T(256)S(1)}, u32[]{:S(2)}) copy-start(f32[256]{0:T(256)S(1)} %add_rsqrt_fusion.1) | copy-start | bytes 3076
  280.2 65.2 %copy-start.44 = (f32[768]{0:T(1024)S(1)}, f32[768]{0:T(1024)}, u32[]{:S(2)}) copy-start(f32[768]{0:T(1024)} %get-tuple-element.735) | copy-start | bytes 9220
  345.5 7.5 slice-start.2
  345.5 5.7 copy-start.34
  345.5 5.7 copy-start.43
  345.5 7.5 slice-start.3
  351.1 4.9 slice-start
  360.6 198.6 %reduce-scatter.8.cloned.1.call-start = ((), (), s32[]{:S(2)}) async-start(), calls=%async_computation.12 | async-start | bytes 2433024 | tf_op jit(solution)/shard_map/reduce_scatter | solution.py:281
  362.6 298.0 %reduce-scatter.10.cloned.1.call-start = ((), (), s32[]{:S(2)}) async-start(), calls=%async_computation.13 | async-start | bytes 9732096 | tf_op jit(solution)/shard_map/reduce_scatter | solution.py:283
  369.6 432.0 %reduce-scatter.12.cloned.1.call-start = ((), (), s32[]{:S(2)}) async-start(), calls=%async_computation.14 | async-start | bytes 9732096 | tf_op jit(solution)/shard_map/reduce_scatter | solution.py:284
  374.4 6.3 copy-start.28
  380.7 546.3 %reduce-scatter.14.cloned.1.call-start = ((), (), s32[]{:S(2)}) async-start(), calls=%async_computation.15 | async-start | bytes 7299072
  380.8 37.2 %copy-start.29 = (f32[2,128,12]{1,0,2:T(2,128)S(1)}, f32[2,128,12]{1,0,2:T(2,128)}, u32[]{:S(2)}) copy-start(f32[2,128,12]{1,0,2:T(2,128)} %copy-done.28) | copy-start | bytes 36868
  512.5 42.5 %copy-start.7 = (f32[256,768]{1,0:T(8,128)S(1)}, f32[256,768]{1,0:T(8,128)}, u32[]{:S(2)}) copy-start(f32[256,768]{1,0:T(8,128)} %copy-done.6) | copy-start | bytes 2359300
  (63 other events, 130.4 us)
Sparse Core Ops, SparseCore 0:
  10.9 62.7 all-gather.9
  77.9 31.7 all-gather.11
  128.7 29.0 all-gather.13
  160.6 54.1 all-gather.15
  217.6 62.5 all-gather.17
  283.0 62.4 all-gather.19
  347.3 31.6 all-gather.21
  380.9 32.8 all-gather.23
  419.6 99.0 reduce-scatter.7
  526.0 134.5 reduce-scatter.9
  667.1 134.4 reduce-scatter.11
  808.6 118.3 reduce-scatter.13
where the time goes:
time: 937 us; the launch traced here: 934 us
  waiting for transfers between devices  555 us (59%)
  blocking collectives  140 us (15%)
  matrix products  108 us (12%)
  local copies, waits for them, and re-layouts  76 us (8%)
  other arithmetic  39 us (4%)
  between operations  14.8 us (2%)
    reduce_scatter x1, waiting for transfers between devices, on_device(): lax.psum_scatter(grad_reduce_local, ('batch', 'seq'), scatter_dimension=0...  141 us
    unnamed x13, waiting for transfers between devices  128 us
    reduce_scatter x1, waiting for transfers between devices, on_device(): lax.psum_scatter(grad_expand_local, ('batch', 'seq'), scatter_dimension=0...  101 us
    unnamed x2, blocking collectives  77.4 us
    all_gather x1, waiting for transfers between devices, gather_attention(): lax.all_gather(joint_weight, ('batch', 'seq'), axis=0, tiled=True)  64.5 us
    all_gather x1, waiting for transfers between devices, gather_feed(): lax.all_gather(expand_weight, ('batch', 'seq'), axis=0, tiled=True)  60.8 us
    all_gather x1, waiting for transfers between devices, gather_feed(): lax.all_gather(reduce_weight, ('batch', 'seq'), axis=0, tiled=True)  59.1 us
    all_gather x1, blocking collectives, gather_attention(): lax.all_gather(vectors, ('batch', 'seq'), axis=1, tiled=True)  42.5 us
  transfers between devices with their start and end apart: 12, of which 6 were waited for; matrix products, arithmetic and copies ran while one was open for 22% of the time, Pallas kernels for 0%

commit v1 on v0

--- a/solution.py
+++ b/solution.py
@@ -14,6 +14,18 @@
 block_limit = 256
 
 
+def collect(array, axis, dim):
+    ways, here = (lax.axis_size(axis), lax.axis_index(axis))
+    grown, reach = (array, 1)
+    while reach < ways:
+        theirs = lax.ppermute(grown, axis, [(d, d ^ reach) for d in range(ways)])
+        mine_first = jnp.concatenate([grown, theirs], axis=dim)
+        theirs_first = jnp.concatenate([theirs, grown], axis=dim)
+        grown = jnp.where(here & reach == 0, mine_first, theirs_first)
+        reach = 2 * reach
+    return grown
+
+
 def layer_norm(residual, norm_gain, norm_shift):
     centered = residual - jnp.mean(residual, axis=-1, keepdims=True)
     inverse = lax.rsqrt(jnp.mean(centered * centered, axis=-1, keepdims=True) + EPSILON)
@@ -73,7 +85,7 @@
 
 def gather_feed(expand_weight, reduce_weight, expand_bias):
     return (
-        lax.all_gather(expand_weight, ("batch", "seq"), axis=0, tiled=True),
+        collect(expand_weight, ("batch", "seq"), 0),
         lax.all_gather(reduce_weight, ("batch", "seq"), axis=0, tiled=True),
         lax.all_gather(expand_bias, ("batch", "seq"), axis=0, tiled=True),
     )

time: 937 us -> 956 us (1.020)
    ppermute x0 -> x5, waiting for transfers between devices: none -> 98.1 us  [collect(): theirs = lax.ppermute(grown, axis, [(d, d ^ reach) for d in range(ways)])]
    all_gather x1 -> x0, waiting for transfers between devices: 60.8 us -> none  [gather_feed(): lax.all_gather(expand_weight, ('batch', 'seq'), axis=0, tiled=True)]
    all_gather x1, waiting for transfers between devices: 59.1 us -> 36.1 us  [gather_feed(): lax.all_gather(reduce_weight, ('batch', 'seq'), axis=0, tiled=True)]
    unnamed x13 -> x12, waiting for transfers between devices: 128 us -> 127 us
  transfers between devices with their start and end apart: 12 -> 16, of which waited for: 6 -> 9; matrix products, arithmetic and copies ran while one was open for 22% -> 22% of each run, Pallas kernels for 0% -> 0%
where the time goes in v1:
time: 956 us; the launch traced here: 953 us
  waiting for transfers between devices  564 us (59%)
  blocking collectives  147 us (15%)
  matrix products  112 us (12%)
  local copies, waits for them, and re-layouts  69.9 us (7%)
  other arithmetic  42.5 us (4%)
  between operations  14.6 us (2%)
    reduce_scatter x1, waiting for transfers between devices, on_device(): lax.psum_scatter(grad_reduce_local, ('batch', 'seq'), scatter_dimension=0...  141 us
    unnamed x12, waiting for transfers between devices  127 us
    ppermute x5, waiting for transfers between devices, collect(): theirs = lax.ppermute(grown, axis, [(d, d ^ reach) for d in range(ways)])  98.1 us
    reduce_scatter x1, waiting for transfers between devices, on_device(): lax.psum_scatter(grad_expand_local, ('batch', 'seq'), scatter_dimension=0...  97.3 us
    unnamed x2, blocking collectives  86.6 us
    all_gather x1, waiting for transfers between devices, gather_attention(): lax.all_gather(joint_weight, ('batch', 'seq'), axis=0, tiled=True)  64.5 us
    all_gather x1, blocking collectives, gather_attention(): lax.all_gather(vectors, ('batch', 'seq'), axis=1, tiled=True)  39.9 us
    all_gather x1, waiting for transfers between devices, gather_feed(): lax.all_gather(reduce_weight, ('batch', 'seq'), axis=0, tiled=True)  36.1 us
  transfers between devices with their start and end apart: 16, of which 9 were waited for; matrix products, arithmetic and copies ran while one was open for 22% of the time, Pallas kernels for 0%

profile of v1, /device:TPU:0, one launch (start us, length us, event | category | flops | bytes accessed | tf_op | source)
XLA Modules:
  0.0 953.4 jit_solution(12444746135876896372)
XLA Ops:
  9.1 64.5 %all-gather.9.cloned.1.call-done = bf16[768,2304]{1,0:T(8,128)(2,1)} async-done(((bf16[24,2304]{1,0:T(8,128)(2,1)}), bf16[768,2304]{1,0:T(8,128)(2,1)}) %all-gather.9.cloned.1.call-update) | async-done | bytes 3538960 | tf_op jit(solution)/shard_map/all_gather | solution.py:80
  77.9 39.9 %all-gather = bf16[32,24,8]{1,2,0:T(8,128)(2,1)S(1)} all-gather(bf16[1,24,8]{1,2,0:T(8,128)(2,1)S(1)} %bitcast.228), channel_id=1, replica_groups=mesh['batch'=4,'seq'=8] {'batch','seq'}, dimensions={0}, use_global_device_ids=true | all-gather | bytes 12672 | tf_op jit(solution)/shard_map/all_gather | solution.py:82
  122.7 13.4 %collective-permute-done.1 = bf16[48,3072]{1,0:T(8,128)(2,1)S(1)} collective-permute-done((bf16[48,3072]{1,0:T(8,128)(2,1)S(1)}, bf16[48,3072]{1,0:T(8,128)(2,1)S(1)}, u32[]{:S(2)}, u32[]{:S(2)}) %collective-permute-start.1) | collective-permute-done | bytes 294944 | tf_op jit(solution)/shard_map/ppermute | solution.py:21
  137.1 22.6 %collective-permute-done.2 = bf16[96,3072]{1,0:T(8,128)(2,1)} collective-permute-done((bf16[96,3072]{1,0:T(8,128)(2,1)S(1)}, bf16[96,3072]{1,0:T(8,128)(2,1)}, u32[]{:S(2)}, u32[]{:S(2)}) %collective-permute-start.2) | collective-permute-done | bytes 589856 | tf_op jit(solution)/shard_map/ppermute | solution.py:21
  162.0 46.4 %all-reduce = bf16[3072]{0:T(1024)(128)(2,1)S(1)} all-reduce(bf16[3072]{0:T(1024)(128)(2,1)S(1)} %dynamic-update-slice), channel_id=1, replica_groups=mesh['batch'=4,'seq'=8] {'batch','seq'}, use_global_device_ids=true, to_apply=%add | all-reduce | flops 3072 | bytes 12288
  217.5 38.2 %while.48 = (s32[]{:T(128)}, f32[2,12,128]{2,1,0:T(8,128)S(1)}, f32[2,12,128]{2,1,0:T(8,128)}, f32[2,128,12,64]{1,3,2,0:T(8,128)}, s32[2]{0:T(128)}, /*index=5*/...) while((s32[]{:T(128)}, f32[2,12,128]{2,1,0:T(8,128)S(1)}, ...), condition=%wide.region_3.4_spmd.clone, body=%wide.region_0.3_spmd.clone.sunk | while | flops 210586368 | bytes 25862536 | solution.py:61
  261.7 61.0 %collective-permute-done.4 = bf16[384,3072]{1,0:T(8,128)(2,1)} collective-permute-done((bf16[384,3072]{1,0:T(8,128)(2,1)}, bf16[384,3072]{1,0:T(8,128)(2,1)}, u32[]{:S(2)}, u32[]{:S(2)}) %collective-permute-start.4) | collective-permute-done | bytes 2359328 | tf_op jit(solution)/shard_map/ppermute | solution.py:21
  322.7 6.6 multiply_convert_fusion.2
  329.4 36.1 %all-gather.17.cloned.1.call-done = bf16[3072,768]{1,0:T(8,128)(2,1)} async-done(((bf16[96,768]{1,0:T(8,128)(2,1)}), bf16[3072,768]{1,0:T(8,128)(2,1)}) %all-gather.17.cloned.1.call-update) | async-done | bytes 4718608 | tf_op jit(solution)/shard_map/all_gather | solution.py:89
  365.5 4.4 fusion.77
  376.0 6.2 multiply_reduce_fusion.1
  386.8 6.7 fusion.72
  399.7 5.1 fusion.68
  404.9 34.7 %while.49 = (s32[]{:T(128)}, f32[2,128,12,64]{1,3,2,0:T(8,128)}, bf16[2,1024,768]{1,2,0:T(8,128)(2,1)}, s32[2]{0:T(128)}, bf16[2,128,12,64]{1,3,2,0:T(8,128)(2,1...) while((s32[]{:T(128)}, f32[2,128,12,64]{1,3,2,0:T(8,128)}, ...), condition=%wide.region_14.15_spmd.clone, body=%wide.region_13.14_spmd.clone.sunk | while | flops 307299072 | bytes 17329384 | solution.py:61
  409.6 3.8 fusion.148
  418.0 4.1 fusion.148
  426.8 4.1 fusion.148
  435.5 4.1 fusion.148
  441.9 10.2 %all_gather.48 = f32[2,1024,12]{1,0,2:T(2,128)} all-gather(f32[2,128,12]{1,0,2:T(2,128)S(1)} %copy-done.30), channel_id=1, replica_groups=mesh['batch'=4,'seq'=8] {'seq'}, dimensions={1}, use_global_device_ids=true | all-gather | bytes 110592 | tf_op jit(solution)/shard_map/all_gather | solution.py:234
  452.1 10.3 %all_gather.46 = f32[2,1024,12]{1,2,0:T(8,128)} all-gather(f32[2,128,12]{1,2,0:T(8,128)} %bitcast.227), channel_id=1, replica_groups=mesh['batch'=4,'seq'=8] {'seq'}, dimensions={1}, use_global_device_ids=true | all-gather | bytes 110592 | tf_op jit(solution)/shard_map/all_gather | solution.py:233
  463.2 57.7 %while.50 = (s32[]{:T(128)}, f32[2,128,12,64]{1,3,2,0:T(8,128)}, f32[2,128,12,64]{1,3,2,0:T(8,128)}, bf16[2,1024,768]{1,2,0:T(8,128)(2,1)}, s32[2]{0:T(128)}, /*...) while((s32[]{:T(128)}, f32[2,128,12,64]{1,3,2,0:T(8,128)}, ...), condition=%wide.region_16.17_spmd.clone, body=%wide.region_15.16_spmd.clone.sunk | while | flops 411500928 | bytes 24602652 | solution.py:61
  469.4 4.7 fusion.157
  483.5 4.9 fusion.157
  498.0 4.9 fusion.157
  512.6 4.9 fusion.157
  524.6 3.9 convolution_bitcast_fusion
  528.5 8.1 copy.96
  537.6 40.2 %all-reduce.3 = (f32[8,768]{1,0:T(8,128)S(1)}, f32[3072]{0:T(1024)S(1)}) all-reduce(f32[8,768]{1,0:T(8,128)S(1)} %stack.35, f32[3072]{0:T(1024)S(1)} %copy-done.43), channel_id=4, replica_groups=mesh['batch'=4,'seq'=8] {'batch','seq'}, use_global_device_ids=true, to_apply=%region_27.28.clone | all-reduce | flops 9216 | bytes 73728
  579.0 4.2 convolution_add_fusion.2
  583.2 97.3 %reduce-scatter.10.cloned.1.call-done = f32[24,3072]{1,0:T(8,128)} async-done(((f32[768,3072]{1,0:T(8,128)}), f32[24,3072]{1,0:T(8,128)}) %reduce-scatter.10.cloned.1.call-update) | async-done | bytes 294928 | tf_op jit(solution)/shard_map/reduce_scatter | solution.py:295
  680.5 140.7 %reduce-scatter.12.cloned.1.call-done = f32[96,768]{1,0:T(8,128)} async-done(((f32[3072,768]{1,0:T(8,128)}), f32[96,768]{1,0:T(8,128)}) %reduce-scatter.12.cloned.1.call-update) | async-done | bytes 294928 | tf_op jit(solution)/shard_map/reduce_scatter | solution.py:296
  821.2 125.6 %reduce-scatter.14.cloned.1.call-done = f32[24,2304]{1,0:T(8,128)} async-done(((f32[768,2304]{1,0:T(8,128)}), f32[24,2304]{1,0:T(8,128)}) %reduce-scatter.14.cloned.1.call-update) | async-done | bytes 221200
  (365 shorter events, 149.3 us)
Async XLA Ops:
  7.2 66.5 %all-gather.9.cloned.1.call-start = ((), (), s32[]{:S(2)}) async-start(), calls=%async_computation.4 | async-start | bytes 3649536 | tf_op jit(solution)/shard_map/all_gather | solution.py:80
  7.9 209.5 %all-gather.11.cloned.1.call-start = ((), (), s32[]{:S(2)}) async-start(), calls=%async_computation.5 | async-start | bytes 3538944 | tf_op jit(solution)/shard_map/all_gather | solution.py:129
  9.1 67.7 %copy-start.9 = (bf16[256,768]{1,0:T(8,128)(2,1)}, bf16[256,768]{1,0:T(8,128)(2,1)S(1)}, u32[]{:S(2)}) copy-start(bf16[256,768]{1,0:T(8,128)(2,1)S(1)} %bitcast_convert_fusion) | copy-start | bytes 1179652
  9.1 68.7 %copy-start.49 = (bf16[8,24]{1,0:T(8,128)(2,1)S(1)}, bf16[8,24]{1,0:T(8,128)(2,1)}, u32[]{:S(2)}) copy-start(bf16[8,24]{1,0:T(8,128)(2,1)} %param.20) | copy-start | bytes 1156
  76.8 44.3 %copy-start.28 = (bf16[24,3072]{1,0:T(8,128)(2,1)S(1)}, bf16[24,3072]{1,0:T(8,128)(2,1)}, u32[]{:S(2)}) copy-start(bf16[24,3072]{1,0:T(8,128)(2,1)} %param.21) | copy-start | bytes 442372
  76.9 41.9 %copy-start.13 = (bf16[256,768]{1,0:T(8,128)(2,1)}, bf16[256,768]{1,0:T(8,128)(2,1)S(1)}, u32[]{:S(2)}) copy-start(bf16[256,768]{1,0:T(8,128)(2,1)S(1)} %slice.73) | copy-start | bytes 1179652
  77.8 139.6 %all-gather.13.cloned.1.call-start = ((), (), s32[]{:S(2)}) async-start(), calls=%async_computation.6 | async-start | bytes 3538944 | tf_op jit(solution)/shard_map/all_gather | solution.py:130
  118.8 91.5 %copy-start.32 = (f32[768]{0:T(1024)}, f32[768]{0:T(1024)S(1)}, u32[]{:S(2)}) copy-start(f32[768]{0:T(1024)S(1)} %get-tuple-element.733) | copy-start | bytes 9220
  118.9 92.2 %copy-start.11 = (bf16[256,768]{1,0:T(8,128)(2,1)}, bf16[256,768]{1,0:T(8,128)(2,1)S(1)}, u32[]{:S(2)}) copy-start(bf16[256,768]{1,0:T(8,128)(2,1)S(1)} %get-tuple-element.821) | copy-start | bytes 1179652
  118.9 42.9 %copy-start.50 = (bf16[96]{0:T(256)(128)(2,1)S(1)}, bf16[96]{0:T(256)(128)(2,1)}, u32[]{:S(2)}) copy-start(bf16[96]{0:T(256)(128)(2,1)} %param.22) | copy-start | bytes 580
  118.9 91.4 %copy-start.4 = (f32[2,128,768]{2,1,0:T(8,128)S(1)}, f32[2,128,768]{2,1,0:T(8,128)}, u32[]{:S(2)}) copy-start(f32[2,128,768]{2,1,0:T(8,128)} %param.16) | copy-start | bytes 2359300
  119.9 139.4 %all-gather.15.cloned.1.call-start = ((), (), s32[]{:S(2)}) async-start(), calls=%async_computation.7 | async-start | bytes 1216512 | tf_op jit(solution)/shard_map/all_gather | solution.py:81
  120.5 245.0 %all-gather.17.cloned.1.call-start = ((), (), s32[]{:S(2)}) async-start(), calls=%async_computation.8 | async-start | bytes 4866048 | tf_op jit(solution)/shard_map/all_gather | solution.py:89
  121.0 342.2 %all-gather.19.cloned.1.call-start = ((), (), s32[]{:S(2)}) async-start(), calls=%async_computation.9 | async-start | bytes 3538944 | tf_op jit(solution)/shard_map/all_gather | solution.py:227
  121.1 1.4 collective-permute-start
  122.6 13.5 %collective-permute-start.1 = (bf16[48,3072]{1,0:T(8,128)(2,1)S(1)}, bf16[48,3072]{1,0:T(8,128)(2,1)S(1)}, u32[]{:S(2)}, u32[]{:S(2)}) collective-permute-start(bf16[48,3072]{1,0:T(8,128)(2,1)S(1)} %maximum_select_fusion.6), channel_id=1, source_target_pairs={{0,2},{1,3},{2,0},{3,1},{4,6},{5,7},{6,4},{7,5},{8,10},{9,11},{10,... | collective-permute-start | bytes 884744 | tf_op jit(solution)/shard_map/ppermute | solution.py:21
  136.3 23.4 %collective-permute-start.2 = (bf16[96,3072]{1,0:T(8,128)(2,1)S(1)}, bf16[96,3072]{1,0:T(8,128)(2,1)}, u32[]{:S(2)}, u32[]{:S(2)}) collective-permute-start(bf16[96,3072]{1,0:T(8,128)(2,1)S(1)} %maximum_select_fusion.5), channel_id=1, source_target_pairs={{0,4},{1,5},{2,6},{3,7},{4,0},{5,1},{6,2},{7,3},{8,12},{9,13},{10,... | collective-permute-start | bytes 1769480 | tf_op jit(solution)/shard_map/ppermute | solution.py:21
  161.6 50.0 %collective-permute-start.3 = (bf16[192,3072]{1,0:T(8,128)(2,1)S(1)}, bf16[192,3072]{1,0:T(8,128)(2,1)}, u32[]{:S(2)}, u32[]{:S(2)}) collective-permute-start(bf16[192,3072]{1,0:T(8,128)(2,1)S(1)} %maximum_select_fusion.2), channel_id=1, source_target_pairs={{0,8},{1,9},{2,10},{3,11},{4,12},{5,13},{6,14},{7,15},{8,0},{9,1},... | collective-permute-start | bytes 3538952 | tf_op jit(solution)/shard_map/ppermute | solution.py:21
  214.7 108.0 %collective-permute-start.4 = (bf16[384,3072]{1,0:T(8,128)(2,1)}, bf16[384,3072]{1,0:T(8,128)(2,1)}, u32[]{:S(2)}, u32[]{:S(2)}) collective-permute-start(bf16[384,3072]{1,0:T(8,128)(2,1)} %maximum_select_fusion.1), channel_id=1, source_target_pairs={{0,16},{1,17},{2,18},{3,19},{4,20},{5,21},{6,22},{7,23},{8,24},{9,... | collective-permute-start | bytes 7077896 | tf_op jit(solution)/shard_map/ppermute | solution.py:21
  217.2 246.0 %all-gather.21.cloned.1.call-start = ((), (), s32[]{:S(2)}) async-start(), calls=%async_computation.10 | async-start | bytes 3538944 | tf_op jit(solution)/shard_map/all_gather | solution.py:230
  255.7 67.0 %copy-start.27 = (f32[768]{0:T(1024)S(1)}, f32[768]{0:T(1024)}, u32[]{:S(2)}) copy-start(f32[768]{0:T(1024)} %get-tuple-element.737) | copy-start | bytes 9220
  255.7 67.0 %copy-start.31 = (f32[768]{0:T(1024)S(1)}, f32[768]{0:T(1024)}, u32[]{:S(2)}) copy-start(f32[768]{0:T(1024)} %get-tuple-element.736) | copy-start | bytes 9220
  255.7 67.0 %copy-start.42 = (f32[3072]{0:T(1024)S(1)}, f32[3072]{0:T(1024)}, u32[]{:S(2)}) copy-start(f32[3072]{0:T(1024)} %convert_element_type.147) | copy-start | bytes 36868
  261.4 120.8 %copy-start.35 = (f32[256]{0:T(256)}, f32[256]{0:T(256)S(1)}, u32[]{:S(2)}) copy-start(f32[256]{0:T(256)S(1)} %broadcast_multiply_fusion.4) | copy-start | bytes 3076
  261.6 120.6 %copy-start.41 = (f32[256]{0:T(256)}, f32[256]{0:T(256)S(1)}, u32[]{:S(2)}) copy-start(f32[256]{0:T(256)S(1)} %add_rsqrt_fusion.1) | copy-start | bytes 3076
  322.7 42.7 %copy-start.46 = (f32[768]{0:T(1024)S(1)}, f32[768]{0:T(1024)}, u32[]{:S(2)}) copy-start(f32[768]{0:T(1024)} %get-tuple-element.735) | copy-start | bytes 9220
  384.6 198.6 %reduce-scatter.8.cloned.1.call-start = ((), (), s32[]{:S(2)}) async-start(), calls=%async_computation.11 | async-start | bytes 2433024 | tf_op jit(solution)/shard_map/reduce_scatter | solution.py:293
  386.6 293.9 %reduce-scatter.10.cloned.1.call-start = ((), (), s32[]{:S(2)}) async-start(), calls=%async_computation.12 | async-start | bytes 9732096 | tf_op jit(solution)/shard_map/reduce_scatter | solution.py:295
  393.6 427.6 %reduce-scatter.12.cloned.1.call-start = ((), (), s32[]{:S(2)}) async-start(), calls=%async_computation.13 | async-start | bytes 9732096 | tf_op jit(solution)/shard_map/reduce_scatter | solution.py:296
  404.8 542.0 %reduce-scatter.14.cloned.1.call-start = ((), (), s32[]{:S(2)}) async-start(), calls=%async_computation.14 | async-start | bytes 7299072
  404.9 37.0 %copy-start.30 = (f32[2,128,12]{1,0,2:T(2,128)S(1)}, f32[2,128,12]{1,0,2:T(2,128)}, u32[]{:S(2)}) copy-start(f32[2,128,12]{1,0,2:T(2,128)} %copy-done.29) | copy-start | bytes 36868
  536.6 42.4 %copy-start.7 = (f32[256,768]{1,0:T(8,128)S(1)}, f32[256,768]{1,0:T(8,128)}, u32[]{:S(2)}) copy-start(f32[256,768]{1,0:T(8,128)} %copy-done.6) | copy-start | bytes 2359300
  (68 other events, 168.7 us)
Sparse Core Ops, SparseCore 0:
  10.9 62.7 all-gather.8
  77.9 31.7 all-gather.10
  120.0 40.5 all-gather.12
  163.3 51.5 all-gather.14
  217.6 147.7 all-gather.16
  367.2 31.6 all-gather.18
  400.7 32.8 all-gather.20
  439.4 99.0 reduce-scatter.7
  546.0 134.4 reduce-scatter.9
  686.8 134.3 reduce-scatter.11
  828.4 118.3 reduce-scatter.13
